TPU v7x, 32 devices: a whole 2x2x4 slice. The times are simulated.
32 devices in a mesh: dp: 4 (over y, x), space: 8 (over z, core).
Axes of the slice: x: 2, y: 2, z: 4, core: 2. Of those that a mesh axis runs over, the one named last changes fastest.
Arguments:
- signal: bfloat16 [4, 512, 64, 1280], P('dp', None, 'space'), may hold values from -6 to 6
- cotangent: bfloat16 [4, 512, 64, 1280], P('dp', None, 'space'), may hold values from -6 to 6
- spec_weight: bfloat16 [2, 20, 20, 73728], P(None, None, None, 'space'), may hold values from -1.25 to 1.25
- point_weight: bfloat16 [20, 20], replicated, may hold values from -1.25 to 1.25
- bias: bfloat16 [20], replicated, may hold values from -3 to 3
Outputs:
- grad_signal: bfloat16 [4, 512, 64, 1280], P('dp', None, 'space')
- spec_grad: float32 [2, 20, 20, 73728], P(None, None, None, ('space', 'dp'))
All inputs are finite; a program needn't handle non-finite values.
Results may differ from a plain program's by a relative error of at most 0.024.
Values may be sent and summed in bfloat16 or wider, within the bound.
No kernel may reach another device: no remote copies, remote signals or barrier semaphores. Data moves between devices by JAX's collectives and lax.ppermute only.
A program may use at most 256 MiB of HBM per device.

v0:
```python
import math
import jax
import jax.numpy as jnp
import ml_dtypes
import numpy as np
from jax import lax
from jax.sharding import PartitionSpec as P

NX = 64
NY = 64
NZ = 32
NT = 16
C = 20
MX = 24
MY = 24
MZ = 16
MT = 8
MZT = 128
BF = ml_dtypes.bfloat16


def retained(mode_count, length):
    positions = np.arange(mode_count)
    return np.where(positions < mode_count // 2, positions, length - mode_count + positions)


def complex_table(mode_count, length):
    freqs = retained(mode_count, length)
    turns = freqs[:, None] * np.arange(length)[None, :] % length
    angles = turns * (2.0 * math.pi / length)
    norm_scale = 1.0 / math.sqrt(length)
    cos_part = np.cos(angles) * norm_scale
    sin_part = np.sin(angles) * norm_scale
    upper_rows = np.stack([cos_part, sin_part], axis=1)
    lower_rows = np.stack([-sin_part, cos_part], axis=1)
    return np.stack([upper_rows, lower_rows], axis=0)


def depth_tables():
    depth_freq = retained(MZ, NZ)
    time_freq = np.arange(MT)
    depth_turns = depth_freq[:, None] * np.arange(NZ)[None, :] % NZ
    time_turns = time_freq[:, None] * np.arange(NT)[None, :] % NT
    turns = depth_turns[:, None, :, None] * NT + time_turns[None, :, None, :] * NZ
    angles = turns * (2.0 * math.pi / (NZ * NT))
    norm_scale = 1.0 / math.sqrt(NZ * NT)
    forward = np.stack([np.cos(angles), -np.sin(angles)], axis=2) * norm_scale
    doubling = np.where(time_freq == 0, 1.0, 2.0)
    inverse = forward * doubling[None, :, None, None, None]
    return (
        forward.reshape(MZT, 2, NZ * NT).astype(BF),
        inverse.reshape(MZT, 2, NZ * NT).astype(BF),
    )


def gelu_slope(pre_act):
    cumulative = 0.5 * (1.0 + lax.erf(pre_act * (1.0 / math.sqrt(2.0))))
    density = jnp.exp(-0.5 * pre_act * pre_act) * (1.0 / math.sqrt(2.0 * math.pi))
    return cumulative + pre_act * density


def block_table(table_y):
    blocks = np.einsum("cd,PjpY->pcYPdj", np.eye(C), table_y)
    return blocks.reshape(2, C * NY, 2 * C * MY).astype(BF)


def dot32(form, left, right):
    return jnp.einsum(form, left, right, preferred_element_type=jnp.float32)


def local(signal, cotangent, spec_weight, point_weight, bias):
    samples, depth_len, x_rows, merged = signal.shape
    depth_np, inverse_np = depth_tables()
    table_y = complex_table(MY, NY)
    table_x = jnp.asarray(complex_table(MX, NX).astype(BF))
    blocks = jnp.asarray(block_table(table_y))
    depth_table = jnp.asarray(depth_np)
    depth_inverse = jnp.asarray(inverse_np)
    point_block = (
        jnp.einsum("co,yz->cyoz", point_weight.astype(jnp.float32), jnp.eye(NY, dtype=jnp.float32))
        .reshape(C * NY, C * NY)
        .astype(jnp.bfloat16)
    )
    bias_row = jnp.repeat(bias.astype(jnp.float32), NY)
    w_real = spec_weight[0]
    w_imag = spec_weight[1]

    def analyse(table, grid_values):
        real = dot32("mz,szxr->smxr", table[:, 0], grid_values).astype(jnp.bfloat16)
        imag = dot32("mz,szxr->smxr", table[:, 1], grid_values).astype(jnp.bfloat16)
        both = dot32("smxr,rK->smxK", real, blocks[0]) + dot32("smxr,rK->smxK", imag, blocks[1])
        both = both.astype(jnp.bfloat16)
        moved = lax.all_to_all(both, "space", split_axis=1, concat_axis=2, tiled=True)
        halves = moved.reshape(samples, moved.shape[1], NX, 2, C * MY)
        total = dot32("Pipx,smxpr->sPmir", table_x, halves).astype(jnp.bfloat16)
        total = total.reshape(samples, 2, -1, MX, C, MY)
        return jnp.transpose(total, (0, 1, 4, 2, 3, 5)).reshape(samples, 2, C, -1)

    def synthesise(table, spectrum):
        unmerged = spectrum.reshape(samples, 2, C, -1, MX, MY)
        moved = jnp.transpose(unmerged, (0, 1, 3, 4, 2, 5)).reshape(samples, 2, -1, MX, C * MY)
        cells = dot32("Pipx,sPmir->smxpr", table_x, moved).astype(jnp.bfloat16)
        cells = cells.reshape(samples, cells.shape[1], NX, 2 * C * MY)
        back = lax.all_to_all(cells, "space", split_axis=2, concat_axis=1, tiled=True)
        real = dot32("smxK,rK->smxr", back, blocks[0]).astype(jnp.bfloat16)
        imag = dot32("smxK,rK->smxr", back, blocks[1]).astype(jnp.bfloat16)
        return dot32("mz,smxr->szxr", table[:, 0], real) + dot32("mz,smxr->szxr", table[:, 1], imag)

    direct = dot32("szxr,rR->szxR", signal, point_block)
    u_hat = analyse(depth_table, signal)
    v_real = dot32("sik,iok->sok", u_hat[:, 0], w_real) - dot32("sik,iok->sok", u_hat[:, 1], w_imag)
    v_imag = dot32("sik,iok->sok", u_hat[:, 1], w_real) + dot32("sik,iok->sok", u_hat[:, 0], w_imag)
    v_hat = jnp.stack([v_real, v_imag], axis=1).astype(jnp.bfloat16)
    pre_act = synthesise(depth_inverse, v_hat) + direct + bias_row
    hidden = (cotangent.astype(jnp.float32) * gelu_slope(pre_act)).astype(jnp.bfloat16)
    h_hat = analyse(depth_inverse, hidden)
    d_real = dot32("sok,iok->sik", h_hat[:, 0], w_real) + dot32("sok,iok->sik", h_hat[:, 1], w_imag)
    d_imag = dot32("sok,iok->sik", h_hat[:, 1], w_real) - dot32("sok,iok->sik", h_hat[:, 0], w_imag)
    d_hat = jnp.stack([d_real, d_imag], axis=1).astype(jnp.bfloat16)
    pointwise = dot32("szxR,rR->szxr", hidden, point_block)
    grad_signal = (synthesise(depth_table, d_hat) + pointwise).astype(jnp.bfloat16)
    u_all = lax.all_to_all(u_hat, "dp", split_axis=3, concat_axis=0, tiled=True)
    h_all = lax.all_to_all(h_hat, "dp", split_axis=3, concat_axis=0, tiled=True)
    u_all = u_all.astype(jnp.float32)
    h_all = h_all.astype(jnp.float32)

    def outer(left, right):
        return jnp.sum(left[:, :, None, :] * right[:, None, :, :], axis=0)

    grad_real = outer(u_all[:, 0], h_all[:, 0]) + outer(u_all[:, 1], h_all[:, 1])
    grad_imag = outer(u_all[:, 0], h_all[:, 1]) - outer(u_all[:, 1], h_all[:, 0])
    return (grad_signal, jnp.stack([grad_real, grad_imag], axis=0))


def solution(mesh):
    return jax.shard_map(
        local,
        mesh=mesh,
        in_specs=(
            P("dp", None, "space", None),
            P("dp", None, "space", None),
            P(None, None, None, "space"),
            P(),
            P(),
        ),
        out_specs=(P("dp", None, "space", None), P(None, None, None, ("space", "dp"))),
        check_vma=False,
    )
```

profile of v0, /device:TPU:0, one launch (start us, length us, event | category | flops | bytes accessed | tf_op | source)
XLA Modules:
  0.0 657.1 jit_solution(13614879044189403960)
XLA Ops:
  0.7 13.3 %fusion.42 = f32[128,8,960]{0,2,1:T(8,128)} fusion(bf16[1280,960,1]{0,1,2:T(8,128)(2,1)} %constant.47, bf16[128,512,1]{1,0,2:T(8,128)(2,1)} %constant.46, bf16[512,8,1280]{2,1,0:T(8,128)(2,1)} %bitcast.305), kind=kOutput, calls=%fused_computation.68 | convolution fusion | flops 3860070400 | bytes 17006592 | tf_op jit(solution)/shard_map/smxr,rK->smxK/dot_general | solution.py:68
  14.0 12.9 %fusion.39 = bf16[1,128,8,960]{1,3,2,0:T(8,128)(2,1)} fusion(f32[128,8,960]{0,2,1:T(8,128)} %fusion.42, bf16[1280,960,1]{0,1,2:T(8,128)(2,1)S(1)} %copy-done.2, bf16[128,512,1]{1,0,2:T(8,128)(2,1)S(1)} %copy-done.5, bf16[512,8,1280]{2,1,0:T(8,128)(2,1)} %bitcast.306), kind=kOutput, calls=%fused_computation.66 | convolution fusion | flops 3862036480 | bytes 18972672 | tf_op jit(solution)/shard_map/smxr,rK->smxK/dot_general | solution.py:68
  31.0 6.5 all-to-all-start
  37.5 29.8 %fusion.66 = (bf16[1,20,20,9216]{3,0,2,1:T(2,128)(2,1)}, bf16[1,20,20,9216]{3,0,2,1:T(2,128)(2,1)}) fusion(bf16[2,20,20,9216]{3,0,2,1:T(2,128)(2,1)} %param.11), kind=kLoop, calls=%fused_computation.96 | loop fusion | bytes 29491200 | tf_op jit(solution)/shard_map/slice | solution.py:86
  67.4 19.2 %all-to-all-done = bf16[1,128,8,960]{3,2,0,1:T(8,128)(2,1)S(1)} async-done(((bf16[1,128,8,960]{3,2,0,1:T(8,128)(2,1)}), bf16[1,128,8,960]{3,2,0,1:T(8,128)(2,1)S(1)}, u32[]{:S(2)}, u32[]{:S(2)}) %all-to-all-start) | async-done | bytes 1966112 | tf_op jit(solution)/shard_map/all_to_all | solution.py:93
  92.3 4.5 reshape.296
  96.8 5.2 copy.261
  102.0 6.2 reshape.297
  110.0 7.8 %copy.295 = bf16[1,2,20,9216]{2,1,0,3:T(2,128)(2,1)} copy(bf16[1,2,20,9216]{3,1,2,0:T(2,128)(2,1)S(1)} %reshape.297) | data formatting | bytes 1474560 | tf_op jit(solution)/shard_map/reshape | solution.py:97
  117.8 11.3 %reshape.360 = bf16[4,2,46080]{2,1,0:T(2,128)(2,1)} reshape(bf16[9216,1,2,20]{3,2,1,0:T(2,128)(2,1)} %bitcast.294) | data formatting | bytes 1474560
  133.3 19.1 %fusion.8 = (f32[9216,20]{0,1:T(8,128)S(1)}, f32[9216,20]{0,1:T(8,128)S(1)}, f32[9216,20]{0,1:T(8,128)S(1)}, f32[9216,20]{0,1:T(8,128)S(1)}) fusion(f32[9216,20]{0,1:T(8,128)S(1)} %get-tuple-element.43, bf16[1,20,20,9216]{3,0,2,1:T(2,128)(2,1)} %get-tuple-element.33, f32[9216,20]{0,1:T(8,128)S(1)} %get-tuple-element.42, ...), kind=kLoop, calls=%fused_computation.19 | loop fusion | flops 36126720 | bytes 19169280 | tf_op jit(solution)/shard_map/sik,iok->sok/dot_general | solution.py:68
  156.6 5.3 stack.23
  164.3 6.4 copy.368
  170.8 5.6 reshape.333
  182.3 4.5 all-to-all-start.1
  186.8 5.0 fusion.23
  191.8 10.0 %reshape.352 = bf16[1280,1280,1]{1,0,2:T(8,128)(2,1)} reshape(bf16[20,64,20,64]{3,2,1,0:T(8,128)(2,1)} %fusion.23) | data formatting | bytes 6553600 | tf_op jit(solution)/shard_map/convert_element_type | solution.py:82
  201.8 8.6 %convert_element_type.187 = bf16[1280,1280]{1,0:T(8,128)(2,1)S(1)} reshape(bf16[20,64,20,64]{3,2,1,0:T(8,128)(2,1)} %fusion.23) | data formatting | bytes 6553600 | tf_op jit(solution)/shard_map/convert_element_type | solution.py:82
  210.4 16.4 %copy.254 = bf16[1,512,8,1280]{1,3,2,0:T(8,128)(2,1)} copy(bf16[1,512,8,1280]{3,2,1,0:T(8,128)(2,1)} %param.10) | data formatting | bytes 20971520 | tf_op args[1]
  227.0 20.6 %fusion.17 = f32[1280,512,8]{1,0,2:T(8,128)} fusion(bf16[512,8,1280]{2,1,0:T(8,128)(2,1)} %bitcast.307, bf16[1280,1280]{1,0:T(8,128)(2,1)S(1)} %convert_element_type.187), kind=kOutput, calls=%fused_computation.34 | convolution fusion | flops 13421772800 | bytes 34734080 | tf_op jit(solution)/shard_map/szxr,rR->szxR/dot_general | solution.py:68
  247.5 14.2 %reshape.361 = bf16[9216,1,2,20]{3,2,1,0:T(2,128)(2,1)} reshape(bf16[4,2,46080]{2,1,0:T(2,128)(2,1)} %copy-done.3) | data formatting | bytes 1474560
  261.7 10.4 %copy.296 = bf16[1,2,20,9216]{3,1,2,0:T(2,128)(2,1)S(1)} copy(bf16[1,2,20,9216]{2,1,0,3:T(2,128)(2,1)} %bitcast.295) | data formatting | bytes 1474560 | tf_op jit(solution)/shard_map/all_to_all | solution.py:122
  273.9 4.3 copy.269
  282.4 11.6 %fusion.33 = f32[8,1280,512]{2,1,0:T(8,128)} fusion(bf16[128,512,1]{1,0,2:T(8,128)(2,1)S(1)} %copy-done.8, bf16[128,8,960]{0,2,1:T(8,128)(2,1)} %copy.270, bf16[1280,960,1]{0,1,2:T(8,128)(2,1)S(1)} %copy-done.1), kind=kOutput, calls=%fused_computation.60 | convolution fusion | flops 3860070400 | bytes 25526272 | tf_op jit(solution)/shard_map/mz,smxr->szxr/dot_general | solution.py:68
  293.9 28.3 %fusion.16 = bf16[512,8,1280]{0,2,1:T(8,128)(2,1)} fusion(f32[1280,512,8]{1,0,2:T(8,128)} %fusion.17, f32[8,1280,512]{2,1,0:T(8,128)} %fusion.33, bf16[128,512,1]{1,0,2:T(8,128)(2,1)S(1)} %copy-done.15, bf16[1,512,8,1280]{1,3,2,0:T(8,128)(2,1)} %copy.254, f32[1280]{0:T(1024)S(1)} %add.90, bf16[128,8,960]{0,2,1:T(8,128)(2,1)} %copy.270, ...), kind=kOutput, calls=%fused_computation.32 | convolution fusion | flops 3933470720 | bytes 67474432 | tf_op jit(solution)/shard_map/mz,smxr->szxr/dot_general | solution.py:68
  322.3 12.8 %fusion.58 = f32[128,8,960]{0,2,1:T(8,128)} fusion(bf16[1280,960,1]{0,1,2:T(8,128)(2,1)S(1)} %copy-done.1, bf16[512,8,1280]{0,2,1:T(8,128)(2,1)} %fusion.16, bf16[128,512,1]{1,0,2:T(8,128)(2,1)S(1)} %copy-done.8), kind=kOutput, calls=%fused_computation.79 | convolution fusion | flops 3860070400 | bytes 17006592 | tf_op jit(solution)/shard_map/smxr,rK->smxK/dot_general | solution.py:68
  335.0 12.9 %fusion.40 = bf16[1,128,8,960]{1,3,2,0:T(8,128)(2,1)S(1)} fusion(f32[128,8,960]{0,2,1:T(8,128)} %fusion.58, bf16[1280,960,1]{0,1,2:T(8,128)(2,1)} %constant.49, bf16[512,8,1280]{0,2,1:T(8,128)(2,1)} %fusion.16, bf16[128,512,1]{1,0,2:T(8,128)(2,1)S(1)} %copy-done.15), kind=kOutput, calls=%fused_computation.67 | convolution fusion | flops 3862036480 | bytes 18972672 | tf_op jit(solution)/shard_map/smxr,rK->smxK/dot_general | solution.py:68
  350.8 5.3 all-to-all-start.2
  358.7 21.4 %fusion.69 = f32[512,8,1280]{0,2,1:T(8,128)} fusion(bf16[1280,1280,1]{1,0,2:T(8,128)(2,1)} %reshape.352, bf16[512,8,1280]{0,2,1:T(8,128)(2,1)} %fusion.16), kind=kOutput, calls=%fused_computation.99 | convolution fusion | flops 13421772800 | bytes 34734080 | tf_op jit(solution)/shard_map/szxR,rR->szxr/dot_general | solution.py:68
  380.1 25.0 %all-to-all-done.2 = bf16[1,128,8,960]{3,2,0,1:T(8,128)(2,1)S(1)} async-done(((bf16[1,128,8,960]{3,2,0,1:T(8,128)(2,1)}), bf16[1,128,8,960]{3,2,0,1:T(8,128)(2,1)S(1)}, u32[]{:S(2)}, u32[]{:S(2)}) %all-to-all-start.2) | async-done | bytes 1966112 | tf_op jit(solution)/shard_map/all_to_all | solution.py:93
  410.9 4.5 reshape.307
  415.4 5.2 copy.282
  420.6 6.2 reshape.308
  427.8 7.8 %copy.297 = bf16[1,2,20,9216]{2,1,0,3:T(2,128)(2,1)} copy(bf16[1,2,20,9216]{3,1,2,0:T(2,128)(2,1)S(1)} %reshape.308) | data formatting | bytes 1474560 | tf_op jit(solution)/shard_map/reshape | solution.py:97
  435.9 11.2 %reshape.362 = bf16[4,2,46080]{2,1,0:T(2,128)(2,1)} reshape(bf16[9216,1,2,20]{3,2,1,0:T(2,128)(2,1)} %bitcast.293) | data formatting | bytes 1474560
  447.1 4.4 all-to-all-start.5
  451.5 22.1 %fusion.12 = (f32[9216,20]{0,1:T(8,128)S(1)}, f32[9216,20]{0,1:T(8,128)S(1)}, f32[9216,20]{0,1:T(8,128)S(1)}, f32[9216,20]{0,1:T(8,128)S(1)}) fusion(f32[9216,20]{0,1:T(8,128)S(1)} %bitcast_convert_fusion.5, bf16[1,20,20,9216]{3,0,2,1:T(2,128)(2,1)} %get-tuple-element.33, f32[9216,20]{0,1:T(8,128)S(1)} %bitcast_convert_fusion.4, ...), kind=kLoop, calls=%fused_computation.23 | loop fusion | flops 36126720 | bytes 19169280 | tf_op jit(solution)/shard_map/sok,iok->sik/dot_general | solution.py:68
  477.6 5.3 stack.26
  485.4 6.4 copy.373
  491.8 5.6 reshape.349
  503.3 4.5 all-to-all-start.3
  507.8 12.7 %reshape.363 = bf16[9216,1,2,20]{3,2,1,0:T(2,128)(2,1)} reshape(bf16[4,2,46080]{2,1,0:T(2,128)(2,1)S(1)} %all-to-all-done.5) | data formatting | bytes 1474560
  520.5 10.0 %copy.298 = bf16[1,2,20,9216]{3,1,2,0:T(2,128)(2,1)S(1)} copy(bf16[1,2,20,9216]{2,1,0,3:T(2,128)(2,1)} %bitcast.296) | data formatting | bytes 1474560 | tf_op jit(solution)/shard_map/all_to_all | solution.py:123
  532.4 40.5 %multiply_reduce_fusion.2 = (f32[20,20,2304]{2,1,0:T(8,128)S(1)}, f32[20,20,2304]{2,1,0:T(8,128)S(1)}, f32[20,20,2304]{2,1,0:T(8,128)S(1)}, f32[20,20,2304]{2,1,0:T(8,128)S(1)}) fusion(f32[4,20,2304]{2,0,1:T(4,128)} %get-tuple-element.37, f32[4,20,2304]{2,0,1:T(4,128)} %get-tuple-element.35, f32[4,20,2304]{2,0,1:T(4,128)} %get-tuple-element.36, ...), kind=kLoop, calls=%fused_computation.30 | loop fusion | flops 25804800 | bytes 17694720 | tf_op jit(solution)/shard_map/reduce_sum | solution.py:128
  581.9 12.3 %copy.300 = f32[2,20,20,2304]{3,0,2,1:T(2,128)} copy(f32[2,20,20,2304]{3,2,1,0:T(8,128)} %pad_maximum_fusion) | data formatting | bytes 14745600
  601.6 13.3 %fusion.34 = f32[8,1280,512]{2,1,0:T(8,128)} fusion(bf16[128,512,1]{1,0,2:T(8,128)(2,1)S(1)} %copy-done.7, bf16[128,8,960]{0,2,1:T(8,128)(2,1)S(1)} %copy.289, bf16[1280,960,1]{0,1,2:T(8,128)(2,1)} %constant.47), kind=kOutput, calls=%fused_computation.61 | convolution fusion | flops 3860070400 | bytes 25526272 | tf_op jit(solution)/shard_map/mz,smxr->szxr/dot_general | solution.py:68
  615.0 25.0 %fusion.6 = bf16[1,512,8,1280]{1,3,2,0:T(8,128)(2,1)} fusion(f32[512,8,1280]{0,2,1:T(8,128)} %fusion.69, f32[8,1280,512]{2,1,0:T(8,128)} %fusion.34, bf16[128,512,1]{1,0,2:T(8,128)(2,1)S(1)} %copy-done.6, bf16[128,8,960]{0,2,1:T(8,128)(2,1)S(1)} %copy.289, bf16[1280,960,1]{0,1,2:T(8,128)(2,1)} %constant.49), kind=kOutput, calls=%fused_computation.16 | convolution fusion | flops 3875799040 | bytes 56983552 | tf_op jit(solution)/shard_map/mz,smxr->szxr/dot_general | solution.py:68
  640.0 16.6 %copy.299 = bf16[1,512,8,1280]{3,2,1,0:T(8,128)(2,1)} copy(bf16[1,512,8,1280]{1,3,2,0:T(8,128)(2,1)} %fusion.6) | data formatting | bytes 20971520
  (80 shorter events, 77.7 us)
Async XLA Ops:
  0.6 13.3 %copy-start.2 = (bf16[1280,960,1]{0,1,2:T(8,128)(2,1)S(1)}, bf16[1280,960,1]{0,1,2:T(8,128)(2,1)}, u32[]{:S(2)}) copy-start(bf16[1280,960,1]{0,1,2:T(8,128)(2,1)} %constant.49) | copy-start | bytes 7372804
  0.6 13.3 %copy-start.5 = (bf16[128,512,1]{1,0,2:T(8,128)(2,1)S(1)}, bf16[128,512,1]{1,0,2:T(8,128)(2,1)}, u32[]{:S(2)}) copy-start(bf16[128,512,1]{1,0,2:T(8,128)(2,1)} %constant.48) | copy-start | bytes 393220
  31.0 55.6 %all-to-all-start = ((bf16[1,128,8,960]{3,2,0,1:T(8,128)(2,1)}), bf16[1,128,8,960]{3,2,0,1:T(8,128)(2,1)S(1)}, u32[]{:S(2)}, u32[]{:S(2)}) async-start(bf16[1,128,8,960]{3,2,0,1:T(8,128)(2,1)} %copy.257), calls=%async_computation | async-start | bytes 4194304 | tf_op jit(solution)/shard_map/all_to_all | solution.py:93
  37.5 29.8 %copy-start.13 = (bf16[20,20]{1,0:T(8,128)(2,1)S(1)}, bf16[20,20]{1,0:T(8,128)(2,1)}, u32[]{:S(2)}) copy-start(bf16[20,20]{1,0:T(8,128)(2,1)} %param.12) | copy-start | bytes 2404
  67.3 24.4 %copy-start.11 = (bf16[2,24,2,64,1]{3,1,2,0,4:T(8,128)(2,1)S(1)}, bf16[2,24,2,64,1]{3,1,2,0,4:T(8,128)(2,1)}, u32[]{:S(2)}) copy-start(bf16[2,24,2,64,1]{3,1,2,0,4:T(8,128)(2,1)} %constant.50) | copy-start | bytes 36868
  117.8 15.2 %copy-start.4 = (bf16[1,1,20,9216]{3,1,2,0:T(2,128)(2,1)S(1)}, bf16[1,1,20,9216]{3,1,2,0:T(2,128)(2,1)}, u32[]{:S(2)}) copy-start(bf16[1,1,20,9216]{3,1,2,0:T(2,128)(2,1)} %get-tuple-element.41) | copy-start | bytes 1105924
  129.1 53.2 %all-to-all-start.4 = ((bf16[4,2,46080]{2,1,0:T(2,128)(2,1)}), bf16[4,2,46080]{2,1,0:T(2,128)(2,1)S(1)}, u32[]{:S(2)}, u32[]{:S(2)}) async-start(bf16[4,2,46080]{2,1,0:T(2,128)(2,1)} %reshape.360), calls=%async_computation.4 | async-start | bytes 1474560 | tf_op jit(solution)/shard_map/all_to_all | solution.py:122
  170.8 5.6 copy-start.9
  182.3 9.6 %copy-start.3 = (bf16[4,2,46080]{2,1,0:T(2,128)(2,1)}, bf16[4,2,46080]{2,1,0:T(2,128)(2,1)S(1)}, u32[]{:S(2)}) copy-start(bf16[4,2,46080]{2,1,0:T(2,128)(2,1)S(1)} %all-to-all-done.4) | copy-start | bytes 2211844
  182.3 91.6 %all-to-all-start.1 = ((bf16[1,16,64,960]{3,1,0,2:T(8,128)(2,1)}), bf16[1,16,64,960]{3,1,0,2:T(8,128)(2,1)}, u32[]{:S(2)}, u32[]{:S(2)}) async-start(bf16[1,16,64,960]{3,1,0,2:T(8,128)(2,1)} %reshape.355), calls=%async_computation.1 | async-start | bytes 4194304 | tf_op jit(solution)/shard_map/all_to_all | solution.py:104
  210.4 16.4 %copy-start.14 = (bf16[20]{0:T(256)(128)(2,1)S(1)}, bf16[20]{0:T(256)(128)(2,1)}, u32[]{:S(2)}) copy-start(bf16[20]{0:T(256)(128)(2,1)} %param.13) | copy-start | bytes 124
  273.9 8.5 %copy-start.1 = (bf16[1280,960,1]{0,1,2:T(8,128)(2,1)S(1)}, bf16[1280,960,1]{0,1,2:T(8,128)(2,1)}, u32[]{:S(2)}) copy-start(bf16[1280,960,1]{0,1,2:T(8,128)(2,1)} %constant.47) | copy-start | bytes 7372804
  273.9 8.5 %copy-start.8 = (bf16[128,512,1]{1,0,2:T(8,128)(2,1)S(1)}, bf16[128,512,1]{1,0,2:T(8,128)(2,1)}, u32[]{:S(2)}) copy-start(bf16[128,512,1]{1,0,2:T(8,128)(2,1)} %constant.53) | copy-start | bytes 393220
  282.3 11.6 %copy-start.15 = (bf16[128,512,1]{1,0,2:T(8,128)(2,1)S(1)}, bf16[128,512,1]{1,0,2:T(8,128)(2,1)}, u32[]{:S(2)}) copy-start(bf16[128,512,1]{1,0,2:T(8,128)(2,1)} %constant.54) | copy-start | bytes 393220
  350.8 54.3 %all-to-all-start.2 = ((bf16[1,128,8,960]{3,2,0,1:T(8,128)(2,1)}), bf16[1,128,8,960]{3,2,0,1:T(8,128)(2,1)S(1)}, u32[]{:S(2)}, u32[]{:S(2)}) async-start(bf16[1,128,8,960]{3,2,0,1:T(8,128)(2,1)} %copy.278), calls=%async_computation.2 | async-start | bytes 4194304 | tf_op jit(solution)/shard_map/all_to_all | solution.py:93
  380.1 30.2 %copy-start.12 = (bf16[2,24,2,64,1]{3,1,2,0,4:T(8,128)(2,1)S(1)}, bf16[2,24,2,64,1]{3,1,2,0,4:T(8,128)(2,1)}, u32[]{:S(2)}) copy-start(bf16[2,24,2,64,1]{3,1,2,0,4:T(8,128)(2,1)} %constant.50) | copy-start | bytes 36868
  447.1 56.2 %all-to-all-start.5 = ((bf16[4,2,46080]{2,1,0:T(2,128)(2,1)}), bf16[4,2,46080]{2,1,0:T(2,128)(2,1)S(1)}, u32[]{:S(2)}, u32[]{:S(2)}) async-start(bf16[4,2,46080]{2,1,0:T(2,128)(2,1)} %reshape.362), calls=%async_computation.5 | async-start | bytes 1474560 | tf_op jit(solution)/shard_map/all_to_all | solution.py:123
  491.8 5.6 copy-start.10
  503.3 90.8 %all-to-all-start.3 = ((bf16[1,16,64,960]{3,1,0,2:T(8,128)(2,1)}), bf16[1,16,64,960]{3,1,0,2:T(8,128)(2,1)}, u32[]{:S(2)}, u32[]{:S(2)}) async-start(bf16[1,16,64,960]{3,1,0,2:T(8,128)(2,1)} %reshape.358), calls=%async_computation.3 | async-start | bytes 4194304 | tf_op jit(solution)/shard_map/all_to_all | solution.py:104
  575.5 2.3 copy-start
  594.1 7.5 %copy-start.7 = (bf16[128,512,1]{1,0,2:T(8,128)(2,1)S(1)}, bf16[128,512,1]{1,0,2:T(8,128)(2,1)}, u32[]{:S(2)}) copy-start(bf16[128,512,1]{1,0,2:T(8,128)(2,1)} %constant.46) | copy-start | bytes 393220
  601.6 13.3 %copy-start.6 = (bf16[128,512,1]{1,0,2:T(8,128)(2,1)S(1)}, bf16[128,512,1]{1,0,2:T(8,128)(2,1)}, u32[]{:S(2)}) copy-start(bf16[128,512,1]{1,0,2:T(8,128)(2,1)} %constant.48) | copy-start | bytes 393220
where the time goes:
time: 668 us; the launch traced here: 657 us
  local copies, waits for them, and re-layouts  306 us (46%)
  matrix products  175 us (26%)
  other arithmetic  101 us (15%)
  waiting for transfers between devices  44.2 us (7%)
  starting transfers between devices  29.2 us (4%)
    dot_general x14, matrix products, dot32(): return jnp.einsum(form, left, right, preferred_element_type=jnp.float32)  175 us
    unnamed x39, local copies, waits for them, and re-layouts  96.5 us
    all_to_all x2, waiting for transfers between devices, analyse(): lax.all_to_all(both, 'space', split_axis=1, concat_axis=2, tiled=True)  44.2 us
    dot_general x2, other arithmetic, dot32(): return jnp.einsum(form, left, right, preferred_element_type=jnp.float32)  41.2 us
    reduce_sum x1, other arithmetic, outer(): return jnp.sum(left[:, :, None, :] * right[:, None, :, :], axis=0)  40.5 us
    another operation x8, local copies, waits for them, and re-layouts  38.5 us
    slice x1, local copies, waits for them, and re-layouts, local(): w_imag = spec_weight[1]  29.8 us
    reshape x4, local copies, waits for them, and re-layouts, analyse(): return jnp.transpose(total, (0, 1, 4, 2, 3, 5)).reshape(samples, 2, C, -1)  27.9 us
  transfers between devices with their start and end apart: 6, of which 2 were waited for; matrix products, arithmetic and copies ran while one was open for 50% of the time, Pallas kernels for 0%

commit v1 on v0

--- a/solution.py
+++ b/solution.py
@@ -17,6 +17,17 @@
 MT = 8
 MZT = 128
 BF = ml_dtypes.bfloat16
+
+
+def cut_along(x, dim, size):
+    before, after = (x.shape[:dim], x.shape[dim + 1 :])
+    return jnp.moveaxis(x.reshape(*before, size, -1, *after), dim, 0)
+
+
+def laid_out(pieces, dim):
+    shape = list(pieces.shape[1:])
+    shape[dim] *= pieces.shape[0]
+    return jnp.moveaxis(pieces, 0, dim).reshape(shape)
 
 
 def retained(mode_count, length):
@@ -120,7 +131,14 @@
     pointwise = dot32("szxR,rR->szxr", hidden, point_block)
     grad_signal = (synthesise(depth_table, d_hat) + pointwise).astype(jnp.bfloat16)
     u_all = lax.all_to_all(u_hat, "dp", split_axis=3, concat_axis=0, tiled=True)
-    h_all = lax.all_to_all(h_hat, "dp", split_axis=3, concat_axis=0, tiled=True)
+    devices, index = (lax.axis_size("dp"), lax.axis_index("dp"))
+    pieces = cut_along(h_hat, 3, devices)
+    outs = [pieces[index]]
+    for lap in range(1, devices):
+        sent = pieces[index ^ lap]
+        outs.append(lax.ppermute(sent, "dp", [(i, i ^ lap) for i in range(devices)]))
+    pieces = jnp.stack(outs)[index ^ jnp.arange(devices)]
+    h_all = laid_out(pieces, 0)
     u_all = u_all.astype(jnp.float32)
     h_all = h_all.astype(jnp.float32)
 

time: 668 us -> 643 us (0.963)
  local copies, waits for them, and re-layouts: 306 us -> 280 us
    unnamed x39 -> x43, local copies, waits for them, and re-layouts: 96.5 us -> 72.6 us
    another operation x8 -> x14, local copies, waits for them, and re-layouts: 38.5 us -> 48.6 us
    all_to_all x1 -> x0, local copies, waits for them, and re-layouts: 9.98 us -> none  [local(): h_all = lax.all_to_all(h_hat, 'dp', split_axis=3, concat_axis=0, tiled=True)]
    reshape x4 -> x3, local copies, waits for them, and re-layouts: 27.9 us -> 20.1 us  [analyse(): return jnp.transpose(total, (0, 1, 4, 2, 3, 5)).reshape(samples, 2, C, -1)]
    transpose x2 -> x3, local copies, waits for them, and re-layouts: 10.4 us -> 13.4 us  [analyse(): return jnp.transpose(total, (0, 1, 4, 2, 3, 5)).reshape(samples, 2, C, -1)]
  transfers between devices with their start and end apart: 6 -> 8, of which waited for: 2 -> 2; matrix products, arithmetic and copies ran while one was open for 50% -> 44% of each run, Pallas kernels for 0% -> 0%
where the time goes in v1:
time: 643 us; the launch traced here: 632 us
  local copies, waits for them, and re-layouts  280 us (44%)
  matrix products  175 us (27%)
  other arithmetic  103 us (16%)
  waiting for transfers between devices  44.2 us (7%)
  starting transfers between devices  28.3 us (4%)
    dot_general x14, matrix products, dot32(): return jnp.einsum(form, left, right, preferred_element_type=jnp.float32)  175 us
    unnamed x43, local copies, waits for them, and re-layouts  72.6 us
    all_to_all x2, waiting for transfers between devices, analyse(): lax.all_to_all(both, 'space', split_axis=1, concat_axis=2, tiled=True)  44.2 us
    dot_general x2, other arithmetic, dot32(): return jnp.einsum(form, left, right, preferred_element_type=jnp.float32)  42.3 us
    another operation x13, local copies, waits for them, and re-layouts  41.7 us
    reduce_sum x1, other arithmetic, outer(): return jnp.sum(left[:, :, None, :] * right[:, None, :, :], axis=0)  40.5 us
    slice x1, local copies, waits for them, and re-layouts, local(): w_imag = spec_weight[1]  29.8 us
    reshape x3, local copies, waits for them, and re-layouts, analyse(): return jnp.transpose(total, (0, 1, 4, 2, 3, 5)).reshape(samples, 2, C, -1)  20.1 us
  transfers between devices with their start and end apart: 8, of which 2 were waited for; matrix products, arithmetic and copies ran while one was open for 44% of the time, Pallas kernels for 0%

profile of v1, /device:TPU:0, one launch (start us, length us, event | category | flops | bytes accessed | tf_op | source)
XLA Modules:
  0.0 632.4 jit_solution(6309069969381444963)
XLA Ops:
  0.7 13.3 %fusion.42 = f32[128,8,960]{0,2,1:T(8,128)} fusion(bf16[1280,960,1]{0,1,2:T(8,128)(2,1)} %constant.64, bf16[128,512,1]{1,0,2:T(8,128)(2,1)} %constant.63, bf16[512,8,1280]{2,1,0:T(8,128)(2,1)} %bitcast.331), kind=kOutput, calls=%fused_computation.69 | convolution fusion | flops 3860070400 | bytes 17006592 | tf_op jit(solution)/shard_map/smxr,rK->smxK/dot_general | solution.py:79
  14.0 12.9 %fusion.39 = bf16[1,128,8,960]{1,3,2,0:T(8,128)(2,1)} fusion(f32[128,8,960]{0,2,1:T(8,128)} %fusion.42, bf16[1280,960,1]{0,1,2:T(8,128)(2,1)S(1)} %copy-done.2, bf16[128,512,1]{1,0,2:T(8,128)(2,1)S(1)} %copy-done.6, bf16[512,8,1280]{2,1,0:T(8,128)(2,1)} %bitcast.332), kind=kOutput, calls=%fused_computation.67 | convolution fusion | flops 3862036480 | bytes 18972672 | tf_op jit(solution)/shard_map/smxr,rK->smxK/dot_general | solution.py:79
  26.9 4.1 copy.285
  31.0 6.6 %all-to-all-start = ((bf16[1,128,8,960]{3,2,0,1:T(8,128)(2,1)}), bf16[1,128,8,960]{3,2,0,1:T(8,128)(2,1)S(1)}, u32[]{:S(2)}, u32[]{:S(2)}) async-start(bf16[1,128,8,960]{3,2,0,1:T(8,128)(2,1)} %copy.285), calls=%async_computation | async-start | bytes 4194304 | tf_op jit(solution)/shard_map/all_to_all | solution.py:104
  37.6 29.8 %fusion.67 = (bf16[1,20,20,9216]{3,0,2,1:T(2,128)(2,1)}, bf16[1,20,20,9216]{3,0,2,1:T(2,128)(2,1)}) fusion(bf16[2,20,20,9216]{3,0,2,1:T(2,128)(2,1)} %param.11), kind=kLoop, calls=%fused_computation.109 | loop fusion | bytes 29491200 | tf_op jit(solution)/shard_map/slice | solution.py:97
  67.4 19.1 %all-to-all-done = bf16[1,128,8,960]{3,2,0,1:T(8,128)(2,1)S(1)} async-done(((bf16[1,128,8,960]{3,2,0,1:T(8,128)(2,1)}), bf16[1,128,8,960]{3,2,0,1:T(8,128)(2,1)S(1)}, u32[]{:S(2)}, u32[]{:S(2)}) %all-to-all-start) | async-done | bytes 1966112 | tf_op jit(solution)/shard_map/all_to_all | solution.py:104
  92.3 4.5 reshape.318
  96.8 5.2 copy.289
  102.0 6.2 reshape.319
  110.1 7.8 %copy.323 = bf16[1,2,20,9216]{2,1,0,3:T(2,128)(2,1)} copy(bf16[1,2,20,9216]{3,1,2,0:T(2,128)(2,1)S(1)} %reshape.319) | data formatting | bytes 1474560 | tf_op jit(solution)/shard_map/reshape | solution.py:108
  117.9 11.2 %reshape.393 = bf16[4,2,46080]{2,1,0:T(2,128)(2,1)} reshape(bf16[9216,1,2,20]{3,2,1,0:T(2,128)(2,1)} %bitcast.314) | data formatting | bytes 1474560
  133.5 19.1 %fusion.8 = (f32[9216,20]{0,1:T(8,128)S(1)}, f32[9216,20]{0,1:T(8,128)S(1)}, f32[9216,20]{0,1:T(8,128)S(1)}, f32[9216,20]{0,1:T(8,128)S(1)}) fusion(f32[9216,20]{0,1:T(8,128)S(1)} %get-tuple-element.47, bf16[1,20,20,9216]{3,0,2,1:T(2,128)(2,1)} %get-tuple-element.33, f32[9216,20]{0,1:T(8,128)S(1)} %get-tuple-element.46, ...), kind=kLoop, calls=%fused_computation.20 | loop fusion | flops 36126720 | bytes 19169280 | tf_op jit(solution)/shard_map/sik,iok->sok/dot_general | solution.py:79
  156.8 5.1 stack.35
  164.3 6.4 %copy.402 = bf16[1,2,16,24,20,24]{5,4,3,1,2,0:T(8,128)(2,1)} copy(bf16[1,2,16,24,20,24]{5,3,2,4,1,0:T(8,128)(2,1)S(1)} %maximum_bitcast_fusion) | data formatting | bytes 1474560 | tf_op jit(solution)/shard_map/reshape.35
  170.7 5.6 reshape.366
  182.2 4.6 all-to-all-start.1
  186.8 5.0 fusion.23
  191.8 10.0 %reshape.385 = bf16[1280,1280,1]{1,0,2:T(8,128)(2,1)} reshape(bf16[20,64,20,64]{3,2,1,0:T(8,128)(2,1)} %fusion.23) | data formatting | bytes 6553600 | tf_op jit(solution)/shard_map/convert_element_type | solution.py:93
  201.7 8.6 %convert_element_type.181 = bf16[1280,1280]{1,0:T(8,128)(2,1)S(1)} reshape(bf16[20,64,20,64]{3,2,1,0:T(8,128)(2,1)} %fusion.23) | data formatting | bytes 6553600 | tf_op jit(solution)/shard_map/convert_element_type | solution.py:93
  210.4 16.4 %copy.282 = bf16[1,512,8,1280]{1,3,2,0:T(8,128)(2,1)} copy(bf16[1,512,8,1280]{3,2,1,0:T(8,128)(2,1)} %param.10) | data formatting | bytes 20971520 | tf_op args[1]
  227.5 20.6 %fusion.17 = f32[1280,512,8]{1,0,2:T(8,128)} fusion(bf16[512,8,1280]{2,1,0:T(8,128)(2,1)} %bitcast.333, bf16[1280,1280]{1,0:T(8,128)(2,1)S(1)} %convert_element_type.181), kind=kOutput, calls=%fused_computation.35 | convolution fusion | flops 13421772800 | bytes 34734080 | tf_op jit(solution)/shard_map/szxr,rR->szxR/dot_general | solution.py:79
  248.2 14.2 %reshape.394 = bf16[9216,1,2,20]{3,2,1,0:T(2,128)(2,1)} reshape(bf16[4,2,46080]{2,1,0:T(2,128)(2,1)} %copy-done.4) | data formatting | bytes 1474560
  262.4 10.4 %copy.324 = bf16[1,2,20,9216]{3,1,2,0:T(2,128)(2,1)S(1)} copy(bf16[1,2,20,9216]{2,1,0,3:T(2,128)(2,1)} %bitcast.315) | data formatting | bytes 1474560 | tf_op jit(solution)/shard_map/all_to_all | solution.py:133
  274.6 4.3 copy.297
  278.9 4.1 copy.298
  283.0 11.6 %fusion.33 = f32[8,1280,512]{2,1,0:T(8,128)} fusion(bf16[128,512,1]{1,0,2:T(8,128)(2,1)S(1)} %copy-done.9, bf16[128,8,960]{0,2,1:T(8,128)(2,1)} %copy.298, bf16[1280,960,1]{0,1,2:T(8,128)(2,1)S(1)} %copy-done.1), kind=kOutput, calls=%fused_computation.61 | convolution fusion | flops 3860070400 | bytes 25526272 | tf_op jit(solution)/shard_map/mz,smxr->szxr/dot_general | solution.py:79
  294.6 28.3 %fusion.16 = bf16[512,8,1280]{0,2,1:T(8,128)(2,1)} fusion(f32[1280,512,8]{1,0,2:T(8,128)} %fusion.17, f32[8,1280,512]{2,1,0:T(8,128)} %fusion.33, bf16[128,512,1]{1,0,2:T(8,128)(2,1)S(1)} %copy-done.16, bf16[1,512,8,1280]{1,3,2,0:T(8,128)(2,1)} %copy.282, f32[1280]{0:T(1024)S(1)} %add.112, bf16[128,8,960]{0,2,1:T(8,128)(2,1)} %copy.298, ...), kind=kOutput, calls=%fused_computation.33 | convolution fusion | flops 3933470720 | bytes 67474432 | tf_op jit(solution)/shard_map/mz,smxr->szxr/dot_general | solution.py:79
  323.0 12.8 %fusion.58 = f32[128,8,960]{0,2,1:T(8,128)} fusion(bf16[1280,960,1]{0,1,2:T(8,128)(2,1)S(1)} %copy-done.1, bf16[512,8,1280]{0,2,1:T(8,128)(2,1)} %fusion.16, bf16[128,512,1]{1,0,2:T(8,128)(2,1)S(1)} %copy-done.9), kind=kOutput, calls=%fused_computation.80 | convolution fusion | flops 3860070400 | bytes 17006592 | tf_op jit(solution)/shard_map/smxr,rK->smxK/dot_general | solution.py:79
  335.7 13.0 %fusion.40 = bf16[1,128,8,960]{1,3,2,0:T(8,128)(2,1)S(1)} fusion(f32[128,8,960]{0,2,1:T(8,128)} %fusion.58, bf16[1280,960,1]{0,1,2:T(8,128)(2,1)} %constant.66, bf16[512,8,1280]{0,2,1:T(8,128)(2,1)} %fusion.16, bf16[128,512,1]{1,0,2:T(8,128)(2,1)S(1)} %copy-done.16), kind=kOutput, calls=%fused_computation.68 | convolution fusion | flops 3862036480 | bytes 18972672 | tf_op jit(solution)/shard_map/smxr,rK->smxK/dot_general | solution.py:79
  351.7 5.1 all-to-all-start.2
  359.3 21.5 %fusion.71 = f32[512,8,1280]{0,2,1:T(8,128)} fusion(bf16[1280,1280,1]{1,0,2:T(8,128)(2,1)} %reshape.385, bf16[512,8,1280]{0,2,1:T(8,128)(2,1)} %fusion.16), kind=kOutput, calls=%fused_computation.113 | convolution fusion | flops 13421772800 | bytes 34734080 | tf_op jit(solution)/shard_map/szxR,rR->szxr/dot_general | solution.py:79
  380.8 25.0 %all-to-all-done.2 = bf16[1,128,8,960]{3,2,0,1:T(8,128)(2,1)S(1)} async-done(((bf16[1,128,8,960]{3,2,0,1:T(8,128)(2,1)}), bf16[1,128,8,960]{3,2,0,1:T(8,128)(2,1)S(1)}, u32[]{:S(2)}, u32[]{:S(2)}) %all-to-all-start.2) | async-done | bytes 1966112 | tf_op jit(solution)/shard_map/all_to_all | solution.py:104
  411.5 4.5 reshape.329
  416.1 5.3 copy.310
  424.3 6.2 reshape.330
  431.8 23.1 %fusion.12 = (f32[9216,20]{0,1:T(8,128)S(1)}, f32[9216,20]{0,1:T(8,128)S(1)}, f32[9216,20]{0,1:T(8,128)S(1)}, f32[9216,20]{0,1:T(8,128)}) fusion(f32[9216,20]{0,1:T(8,128)S(1)} %bitcast_convert_fusion.5, bf16[1,20,20,9216]{3,0,2,1:T(2,128)(2,1)} %get-tuple-element.33, f32[9216,20]{0,1:T(8,128)S(1)} %bitcast_convert_fusion.4, ...), kind=kLoop, calls=%fused_computation.24 | loop fusion | flops 36126720 | bytes 19169280 | tf_op jit(solution)/shard_map/sok,iok->sik/dot_general | solution.py:79
  459.4 4.4 stack.38
  463.8 7.0 %reshape_reshape.3 = bf16[1,2,20,4,2304]{4,3,2,1,0:T(4,128)(2,1)S(1)} reshape(bf16[1,2,20,16,24,24]{5,4,3,2,1,0:T(8,128)(2,1)} %copy.325) | data formatting | bytes 1474560 | tf_op jit(solution)/shard_map/reshape;reshape | solution.py:24
  478.2 6.4 %copy.407 = bf16[1,2,16,24,20,24]{5,4,3,1,2,0:T(8,128)(2,1)} copy(bf16[1,2,16,24,20,24]{5,3,2,4,1,0:T(8,128)(2,1)S(1)} %maximum_bitcast_fusion.1) | data formatting | bytes 1474560 | tf_op jit(solution)/shard_map/reshape.67
  484.6 5.7 reshape.382
  496.3 4.3 all-to-all-start.3
  507.6 40.5 %multiply_reduce_fusion.2 = (f32[20,20,2304]{2,1,0:T(8,128)S(1)}, f32[20,20,2304]{2,1,0:T(8,128)S(1)}, f32[20,20,2304]{2,1,0:T(8,128)S(1)}, f32[20,20,2304]{2,1,0:T(8,128)S(1)}) fusion(f32[4,20,2304]{2,0,1:T(4,128)} %bitcast.323, f32[4,20,2304]{2,0,1:T(4,128)} %get-tuple-element.35, f32[4,20,2304]{2,0,1:T(4,128)} %bitcast.324, ...), kind=kLoop, calls=%fused_computation.31 | loop fusion | flops 25804800 | bytes 17694720 | tf_op jit(solution)/shard_map/reduce_sum | solution.py:146
  553.0 4.1 pad_maximum_fusion
  557.1 12.3 %copy.334 = f32[2,20,20,2304]{3,0,2,1:T(2,128)} copy(f32[2,20,20,2304]{3,2,1,0:T(8,128)} %pad_maximum_fusion) | data formatting | bytes 14745600
  569.4 4.2 copy.316
  576.9 13.4 %fusion.34 = f32[8,1280,512]{2,1,0:T(8,128)} fusion(bf16[128,512,1]{1,0,2:T(8,128)(2,1)S(1)} %copy-done.8, bf16[128,8,960]{0,2,1:T(8,128)(2,1)S(1)} %copy.317, bf16[1280,960,1]{0,1,2:T(8,128)(2,1)} %constant.64), kind=kOutput, calls=%fused_computation.62 | convolution fusion | flops 3860070400 | bytes 25526272 | tf_op jit(solution)/shard_map/mz,smxr->szxr/dot_general | solution.py:79
  590.3 25.0 %fusion.6 = bf16[1,512,8,1280]{1,3,2,0:T(8,128)(2,1)} fusion(f32[512,8,1280]{0,2,1:T(8,128)} %fusion.71, f32[8,1280,512]{2,1,0:T(8,128)} %fusion.34, bf16[128,512,1]{1,0,2:T(8,128)(2,1)S(1)} %copy-done.7, bf16[128,8,960]{0,2,1:T(8,128)(2,1)S(1)} %copy.317, bf16[1280,960,1]{0,1,2:T(8,128)(2,1)} %constant.66), kind=kOutput, calls=%fused_computation.17 | convolution fusion | flops 3875799040 | bytes 56983552 | tf_op jit(solution)/shard_map/mz,smxr->szxr/dot_general | solution.py:79
  615.3 16.6 %copy.333 = bf16[1,512,8,1280]{3,2,1,0:T(8,128)(2,1)} copy(bf16[1,512,8,1280]{1,3,2,0:T(8,128)(2,1)} %fusion.6) | data formatting | bytes 20971520
  (99 shorter events, 75.1 us)
Async XLA Ops:
  0.6 13.3 %copy-start.2 = (bf16[1280,960,1]{0,1,2:T(8,128)(2,1)S(1)}, bf16[1280,960,1]{0,1,2:T(8,128)(2,1)}, u32[]{:S(2)}) copy-start(bf16[1280,960,1]{0,1,2:T(8,128)(2,1)} %constant.66) | copy-start | bytes 7372804
  0.6 13.3 %copy-start.6 = (bf16[128,512,1]{1,0,2:T(8,128)(2,1)S(1)}, bf16[128,512,1]{1,0,2:T(8,128)(2,1)}, u32[]{:S(2)}) copy-start(bf16[128,512,1]{1,0,2:T(8,128)(2,1)} %constant.65) | copy-start | bytes 393220
  31.0 55.6 %all-to-all-start = ((bf16[1,128,8,960]{3,2,0,1:T(8,128)(2,1)}), bf16[1,128,8,960]{3,2,0,1:T(8,128)(2,1)S(1)}, u32[]{:S(2)}, u32[]{:S(2)}) async-start(bf16[1,128,8,960]{3,2,0,1:T(8,128)(2,1)} %copy.285), calls=%async_computation | async-start | bytes 4194304 | tf_op jit(solution)/shard_map/all_to_all | solution.py:104
  37.6 29.8 %copy-start.14 = (bf16[20,20]{1,0:T(8,128)(2,1)S(1)}, bf16[20,20]{1,0:T(8,128)(2,1)}, u32[]{:S(2)}) copy-start(bf16[20,20]{1,0:T(8,128)(2,1)} %param.12) | copy-start | bytes 2404
  67.4 24.3 %copy-start.12 = (bf16[2,24,2,64,1]{3,1,2,0,4:T(8,128)(2,1)S(1)}, bf16[2,24,2,64,1]{3,1,2,0,4:T(8,128)(2,1)}, u32[]{:S(2)}) copy-start(bf16[2,24,2,64,1]{3,1,2,0,4:T(8,128)(2,1)} %constant.67) | copy-start | bytes 36868
  117.9 15.3 %copy-start.5 = (bf16[1,1,20,9216]{3,1,2,0:T(2,128)(2,1)S(1)}, bf16[1,1,20,9216]{3,1,2,0:T(2,128)(2,1)}, u32[]{:S(2)}) copy-start(bf16[1,1,20,9216]{3,1,2,0:T(2,128)(2,1)} %get-tuple-element.45) | copy-start | bytes 1105924
  129.1 53.1 %all-to-all-start.4 = ((bf16[4,2,46080]{2,1,0:T(2,128)(2,1)}), bf16[4,2,46080]{2,1,0:T(2,128)(2,1)S(1)}, u32[]{:S(2)}, u32[]{:S(2)}) async-start(bf16[4,2,46080]{2,1,0:T(2,128)(2,1)} %reshape.393), calls=%async_computation.4 | async-start | bytes 1474560 | tf_op jit(solution)/shard_map/all_to_all | solution.py:133
  170.7 5.6 copy-start.10
  182.2 9.6 %copy-start.4 = (bf16[4,2,46080]{2,1,0:T(2,128)(2,1)}, bf16[4,2,46080]{2,1,0:T(2,128)(2,1)S(1)}, u32[]{:S(2)}) copy-start(bf16[4,2,46080]{2,1,0:T(2,128)(2,1)S(1)} %all-to-all-done.4) | copy-start | bytes 2211844
  182.2 92.4 %all-to-all-start.1 = ((bf16[1,16,64,960]{3,1,0,2:T(8,128)(2,1)}), bf16[1,16,64,960]{3,1,0,2:T(8,128)(2,1)}, u32[]{:S(2)}, u32[]{:S(2)}) async-start(bf16[1,16,64,960]{3,1,0,2:T(8,128)(2,1)} %reshape.388), calls=%async_computation.1 | async-start | bytes 4194304 | tf_op jit(solution)/shard_map/all_to_all | solution.py:115
  210.4 16.4 %copy-start.15 = (bf16[20]{0:T(256)(128)(2,1)S(1)}, bf16[20]{0:T(256)(128)(2,1)}, u32[]{:S(2)}) copy-start(bf16[20]{0:T(256)(128)(2,1)} %param.13) | copy-start | bytes 124
  274.6 8.5 %copy-start.1 = (bf16[1280,960,1]{0,1,2:T(8,128)(2,1)S(1)}, bf16[1280,960,1]{0,1,2:T(8,128)(2,1)}, u32[]{:S(2)}) copy-start(bf16[1280,960,1]{0,1,2:T(8,128)(2,1)} %constant.64) | copy-start | bytes 7372804
  274.6 8.5 %copy-start.9 = (bf16[128,512,1]{1,0,2:T(8,128)(2,1)S(1)}, bf16[128,512,1]{1,0,2:T(8,128)(2,1)}, u32[]{:S(2)}) copy-start(bf16[128,512,1]{1,0,2:T(8,128)(2,1)} %constant.70) | copy-start | bytes 393220
  283.0 11.6 %copy-start.16 = (bf16[128,512,1]{1,0,2:T(8,128)(2,1)S(1)}, bf16[128,512,1]{1,0,2:T(8,128)(2,1)}, u32[]{:S(2)}) copy-start(bf16[128,512,1]{1,0,2:T(8,128)(2,1)} %constant.71) | copy-start | bytes 393220
  351.7 54.1 %all-to-all-start.2 = ((bf16[1,128,8,960]{3,2,0,1:T(8,128)(2,1)}), bf16[1,128,8,960]{3,2,0,1:T(8,128)(2,1)S(1)}, u32[]{:S(2)}, u32[]{:S(2)}) async-start(bf16[1,128,8,960]{3,2,0,1:T(8,128)(2,1)} %copy.306), calls=%async_computation.2 | async-start | bytes 4194304 | tf_op jit(solution)/shard_map/all_to_all | solution.py:104
  380.8 30.2 %copy-start.13 = (bf16[2,24,2,64,1]{3,1,2,0,4:T(8,128)(2,1)S(1)}, bf16[2,24,2,64,1]{3,1,2,0,4:T(8,128)(2,1)}, u32[]{:S(2)}) copy-start(bf16[2,24,2,64,1]{3,1,2,0,4:T(8,128)(2,1)} %constant.67) | copy-start | bytes 36868
  416.1 5.4 slice-start
  416.1 5.4 slice-start.1
  470.8 6.5 %copy-start.3 = (bf16[1,1,20,16,24,24]{5,4,3,2,1,0:T(8,128)(2,1)S(1)}, bf16[1,1,20,16,24,24]{5,4,3,2,1,0:T(8,128)(2,1)}, u32[]{:S(2)}) copy-start(bf16[1,1,20,16,24,24]{5,4,3,2,1,0:T(8,128)(2,1)} %stack.38) | copy-start | bytes 1105924
  472.6 28.3 %collective-permute-start.2 = (bf16[1,2,20,2304]{3,1,2,0:T(2,128)(2,1)S(1)}, bf16[1,2,20,2304]{3,1,2,0:T(2,128)(2,1)S(1)}, u32[]{:S(2)}, u32[]{:S(2)}) collective-permute-start(bf16[1,2,20,2304]{3,1,2,0:T(2,128)(2,1)S(1)} %bitcast.328), channel_id=1, source_target_pairs={{0,24},{8,16},{16,8},{24,0},{1,25},{9,17},{17,9},{25,1},{2,26},{10... | collective-permute-start | bytes 552968 | tf_op jit(solution)/shard_map/ppermute | solution.py:139
  475.7 25.1 %collective-permute-start.1 = (bf16[1,2,20,2304]{3,1,2,0:T(2,128)(2,1)S(1)}, bf16[1,2,20,2304]{3,1,2,0:T(2,128)(2,1)S(1)}, u32[]{:S(2)}, u32[]{:S(2)}) collective-permute-start(bf16[1,2,20,2304]{3,1,2,0:T(2,128)(2,1)S(1)} %bitcast.329), channel_id=1, source_target_pairs={{0,16},{8,24},{16,0},{24,8},{1,17},{9,25},{17,1},{25,9},{2,18},{10... | collective-permute-start | bytes 552968 | tf_op jit(solution)/shard_map/ppermute | solution.py:139
  477.2 23.6 %collective-permute-start = (bf16[1,2,20,2304]{3,1,2,0:T(2,128)(2,1)}, bf16[1,2,20,2304]{3,1,2,0:T(2,128)(2,1)S(1)}, u32[]{:S(2)}, u32[]{:S(2)}) collective-permute-start(bf16[1,2,20,2304]{3,1,2,0:T(2,128)(2,1)} %bitcast.307), channel_id=1, source_target_pairs={{0,8},{8,0},{16,24},{24,16},{1,9},{9,1},{17,25},{25,17},{2,10},{10... | collective-permute-start | bytes 552968 | tf_op jit(solution)/shard_map/ppermute | solution.py:139
  484.6 5.7 copy-start.11
  496.3 73.1 %all-to-all-start.3 = ((bf16[1,16,64,960]{3,1,0,2:T(8,128)(2,1)}), bf16[1,16,64,960]{3,1,0,2:T(8,128)(2,1)}, u32[]{:S(2)}, u32[]{:S(2)}) async-start(bf16[1,16,64,960]{3,1,0,2:T(8,128)(2,1)} %reshape.391), calls=%async_computation.3 | async-start | bytes 4194304 | tf_op jit(solution)/shard_map/all_to_all | solution.py:115
  550.7 2.3 copy-start
  569.3 7.5 %copy-start.8 = (bf16[128,512,1]{1,0,2:T(8,128)(2,1)S(1)}, bf16[128,512,1]{1,0,2:T(8,128)(2,1)}, u32[]{:S(2)}) copy-start(bf16[128,512,1]{1,0,2:T(8,128)(2,1)} %constant.63) | copy-start | bytes 393220
  576.8 13.4 %copy-start.7 = (bf16[128,512,1]{1,0,2:T(8,128)(2,1)S(1)}, bf16[128,512,1]{1,0,2:T(8,128)(2,1)}, u32[]{:S(2)}) copy-start(bf16[128,512,1]{1,0,2:T(8,128)(2,1)} %constant.65) | copy-start | bytes 393220
